TPU v7x, 256 devices: a whole 4x4x8 slice. The times are simulated.
256 devices in a mesh: clu: 32 (over x, y, core), sub: 8 (over z).
Axes of the slice: x: 4, y: 4, z: 8, core: 2. Of those that a mesh axis runs over, the one named last changes fastest.
Arguments:
- load_cases: float32 [128, 393216], P(None, ('clu', 'sub')), may hold values from -90 to 90
- initial: float32 [128, 393216], P(None, ('clu', 'sub')), may hold values from -6 to 6
- dual_blocks: bfloat16 [393216, 1536], P(('clu', 'sub')), may hold values from -1 to 3, as said below
- dirichlet: bfloat16 [393216, 1536], P(('clu', 'sub')), may hold values from -1 to 3, as said below
- rigid_modes: float32 [16384, 1536], P(('clu', 'sub')), may hold values from -1 to 1
- coarse_inverse: float32 [16384, 512], P(('clu', 'sub')), may hold values from -2 to 2, as said below
- face_block: int32 [256, 12], P(('clu', 'sub')), may hold values from 0 to 11, each once within a row
- active: int32 [256, 4], P(('clu', 'sub')), may hold values from 0 to 1, as said below
- membership: int32 [256], P('clu'), may hold values from 0 to 1
Outputs:
- multipliers: float32 [128, 393216], P(None, ('clu', 'sub'))
- residual: float32 [128, 393216], P(None, ('clu', 'sub'))
Inputs may be any that keep to these rules, and one draw needn't show every extreme that they name: active[s, g] equals active[p, g] for the partner p of subdomain s in colour g. `coarse_inverse`: each cluster's 512 rows form the inverse of the symmetric positive definite matrix C C^T + 0.5 I, where C stacks the rigid_modes rows of the cluster's subdomains. `dual_blocks`: each subdomain's block is symmetric. `dirichlet`: each subdomain's block is symmetric.
All inputs are finite; a program needn't handle non-finite values.
Results may differ from a plain program's by a relative error of at most 0.0022.
Values sent between devices are 32-bit elements; how exact they have to be, the bound alone decides.
No kernel may reach another device: no remote copies, remote signals or barrier semaphores. Data moves between devices by JAX's collectives and lax.ppermute only.
A program may use at most 64 MiB of HBM per device.

v0:
```python
import jax
import jax.numpy as jnp
from jax import lax
from jax.sharding import PartitionSpec as P

BLK = 128
E = 64
NCOL = 4
ITERS = 3
HIGH = lax.Precision.HIGHEST


def from_partner(value, axis, bit):
    mask = 2**bit
    pairs = [(source, source ^ mask) for source in range(lax.axis_size(axis))]
    return lax.ppermute(value, axis, pairs)


def on_device(
    load_cases,
    initial,
    dual_blocks,
    dirichlet,
    rigid_modes,
    coarse_inverse,
    face_block,
    active,
    membership,
):
    cases = load_cases.shape[0]
    blocks = dual_blocks.shape[0] // BLK
    per_colour = blocks // NCOL
    onehot = (face_block[0][:, None] == jnp.arange(blocks)[None, :]).astype(jnp.float32)
    edge_gates = active[0].astype(jnp.float32)
    own_index = lax.axis_index("sub")
    my_group = lax.dynamic_slice_in_dim(membership, own_index, 1)[0]
    same_group = (membership == my_group).astype(jnp.float32)

    def apply_local(vector, matrix):
        return jnp.dot(vector.astype(jnp.bfloat16), matrix, preferred_element_type=jnp.float32)

    def assemble(product):
        blocked = product.reshape(cases, blocks, BLK)
        slot_vals = jnp.einsum("jq,kqb->kjb", onehot, blocked, precision=HIGH)
        received = []
        for colour in range(NCOL - 1):
            outgoing = slot_vals[:, colour * per_colour : (colour + 1) * per_colour, :]
            incoming = from_partner(outgoing, "clu", colour)
            received.append(incoming * edge_gates[colour])
        outgoing_last = slot_vals[:, (NCOL - 1) * per_colour :, :]
        incoming_last = from_partner(outgoing_last, "sub", 0)
        received.append(incoming_last * edge_gates[NCOL - 1])
        joined = jnp.concatenate(received, axis=1)
        added = jnp.einsum("jq,kjb->kqb", onehot, joined, precision=HIGH)
        return product + added.reshape(cases, blocks * BLK)

    def coarse(vector):
        coeffs = jnp.einsum("em,km->ek", rigid_modes, vector, precision=HIGH)
        flat = coeffs.reshape(1, E * cases)
        piece = lax.all_gather(flat, "sub", axis=0, tiled=True)
        count = piece.shape[0]
        masked = (piece.reshape(count, E, cases) * same_group[:, None, None]).reshape(
            count * E, cases
        )
        amounts = jnp.dot(coarse_inverse, masked, precision=HIGH)
        correction = jnp.einsum("ek,em->km", amounts, rigid_modes, precision=HIGH)
        return vector - correction

    residual = coarse(load_cases - assemble(apply_local(initial, dual_blocks)))
    multipliers = initial
    for step in range(ITERS):
        search = coarse(assemble(apply_local(residual, dirichlet)))
        image = coarse(assemble(apply_local(search, dual_blocks)))
        cross_sum = jnp.sum(residual * image, axis=1)
        image_sum = jnp.sum(image * image, axis=1)
        cross_all, image_all = lax.psum((cross_sum, image_sum), ("clu", "sub"))
        step_len = cross_all / (image_all + 1e-06)
        multipliers = multipliers + step_len[:, None] * search
        residual = residual - step_len[:, None] * image
    return (multipliers, residual)


def solution(mesh):
    in_specs = (
        P(None, ("clu", "sub")),
        P(None, ("clu", "sub")),
        P(("clu", "sub"), None),
        P(("clu", "sub"), None),
        P(("clu", "sub"), None),
        P(("clu", "sub"), None),
        P(("clu", "sub"), None),
        P(("clu", "sub"), None),
        P("clu"),
    )
    out_specs = (P(None, ("clu", "sub")), P(None, ("clu", "sub")))
    return jax.shard_map(
        on_device, mesh=mesh, in_specs=in_specs, out_specs=out_specs, check_vma=False
    )
```

profile of v0, /device:TPU:1, one launch (start us, length us, event | category | flops | bytes accessed | tf_op | source)
XLA Modules:
  0.0 650.1 jit_solution(13790412827187783038)
XLA Ops:
  0.7 3.4 fusion.61
  5.7 3.3 collective-permute-start
  9.0 2.8 collective-permute-start.2
  18.8 5.1 collective-permute-done.1
  30.4 22.0 %all-gather = f32[8,1,8192]{2,1,0:T(1,128)S(1)} all-gather(f32[1,1,8192]{2,1,0:T(1,128)S(1)} %bitcast.168), channel_id=1, replica_groups=mesh['clu'=32,'sub'=8] {'sub'}, dimensions={0}, use_global_device_ids=true | all-gather | bytes 294912 | tf_op jit(solution)/shard_map/all_gather | solution.py:60
  54.8 3.1 fusion.59
  61.6 7.0 %collective-permute-start.4 = (f32[128,3,128]{2,1,0:T(4,128)S(1)}, f32[128,3,128]{2,1,0:T(4,128)S(1)}, u32[]{:S(2)}, u32[]{:S(2)}) collective-permute-start(f32[128,3,128]{2,1,0:T(4,128)S(1)} %get-tuple-element.34), channel_id=1, source_target_pairs={{0,8},{8,0},{16,24},{24,16},{32,40},{40,32},{48,56},{56,48},{64,72... | collective-permute-start | bytes 589832 | tf_op jit(solution)/shard_map/ppermute | solution.py:16
  71.9 4.5 collective-permute-done.7
  79.0 3.3 collective-permute-done.5
  90.0 19.1 %all-gather.1 = f32[8,1,8192]{2,1,0:T(1,128)S(1)} all-gather(f32[1,1,8192]{2,1,0:T(1,128)S(1)} %bitcast.169), channel_id=1, replica_groups=mesh['clu'=32,'sub'=8] {'sub'}, dimensions={0}, use_global_device_ids=true | all-gather | bytes 294912 | tf_op jit(solution)/shard_map/all_gather | solution.py:60
  110.3 3.1 fusion.57
  114.6 2.5 copy.64
  119.2 6.9 %collective-permute-start.8 = (f32[128,3,128]{2,1,0:T(4,128)S(1)}, f32[128,3,128]{2,1,0:T(4,128)S(1)}, u32[]{:S(2)}, u32[]{:S(2)}) collective-permute-start(f32[128,3,128]{2,1,0:T(4,128)S(1)} %get-tuple-element.30), channel_id=1, source_target_pairs={{0,8},{8,0},{16,24},{24,16},{32,40},{40,32},{48,56},{56,48},{64,72... | collective-permute-start | bytes 589832 | tf_op jit(solution)/shard_map/ppermute | solution.py:16
  126.1 3.5 collective-permute-start.10
  130.3 3.5 collective-permute-done.11
  136.5 3.9 collective-permute-done.9
  143.2 2.4 copy.66
  150.1 18.5 %all-gather.2 = f32[8,1,8192]{2,1,0:T(1,128)S(1)} all-gather(f32[1,1,8192]{2,1,0:T(1,128)S(1)} %bitcast.170), channel_id=1, replica_groups=mesh['clu'=32,'sub'=8] {'sub'}, dimensions={0}, use_global_device_ids=true | all-gather | bytes 294912 | tf_op jit(solution)/shard_map/all_gather | solution.py:60
  170.8 81.3 %all-reduce.2 = (f32[128]{0:T(128)S(1)}, f32[128]{0:T(128)S(1)}) all-reduce(f32[128]{0:T(128)S(1)} %get-tuple-element.7, f32[128]{0:T(128)S(1)} %get-tuple-element.6), channel_id=1, replica_groups=mesh['clu'=32,'sub'=8] {'clu','sub'}, use_global_device_ids=true, to_apply=%region_1.0 | all-reduce | flops 256 | bytes 2048 | tf_op jit(solution)/shard_map/psum | solution.py:76
  253.4 3.1 fusion.55
  257.6 2.5 copy.69
  267.4 3.4 collective-permute-done.15
  273.9 4.4 collective-permute-done.13
  281.1 2.4 copy.71
  287.9 19.2 %all-gather.3 = f32[8,1,8192]{2,1,0:T(1,128)S(1)} all-gather(f32[1,1,8192]{2,1,0:T(1,128)S(1)} %bitcast.171), channel_id=1, replica_groups=mesh['clu'=32,'sub'=8] {'sub'}, dimensions={0}, use_global_device_ids=true | all-gather | bytes 294912 | tf_op jit(solution)/shard_map/all_gather | solution.py:60
  308.3 3.1 fusion.53
  312.6 2.5 copy.74
  317.1 7.0 %collective-permute-start.16 = (f32[128,3,128]{2,1,0:T(4,128)S(1)}, f32[128,3,128]{2,1,0:T(4,128)S(1)}, u32[]{:S(2)}, u32[]{:S(2)}) collective-permute-start(f32[128,3,128]{2,1,0:T(4,128)S(1)} %get-tuple-element.22), channel_id=1, source_target_pairs={{0,8},{8,0},{16,24},{24,16},{32,40},{40,32},{48,56},{56,48},{64,72... | collective-permute-start | bytes 589832 | tf_op jit(solution)/shard_map/ppermute | solution.py:16
  327.0 4.9 collective-permute-done.19
  334.0 3.4 collective-permute-done.17
  340.2 2.4 copy.76
  347.0 18.4 %all-gather.4 = f32[8,1,8192]{2,1,0:T(1,128)S(1)} all-gather(f32[1,1,8192]{2,1,0:T(1,128)S(1)} %bitcast.172), channel_id=1, replica_groups=mesh['clu'=32,'sub'=8] {'sub'}, dimensions={0}, use_global_device_ids=true | all-gather | bytes 294912 | tf_op jit(solution)/shard_map/all_gather | solution.py:60
  368.5 80.5 %all-reduce.1 = (f32[128]{0:T(128)S(1)}, f32[128]{0:T(128)S(1)}) all-reduce(f32[128]{0:T(128)S(1)} %get-tuple-element.5, f32[128]{0:T(128)S(1)} %get-tuple-element.4), channel_id=1, replica_groups=mesh['clu'=32,'sub'=8] {'clu','sub'}, use_global_device_ids=true, to_apply=%region_5.0 | all-reduce | flops 256 | bytes 2048 | tf_op jit(solution)/shard_map/psum | solution.py:76
  450.3 3.1 fusion.51
  454.6 2.5 copy.79
  463.0 4.9 collective-permute-done.23
  471.0 2.7 collective-permute-done.21
  476.6 2.4 copy.81
  483.4 19.4 %all-gather.5 = f32[8,1,8192]{2,1,0:T(1,128)S(1)} all-gather(f32[1,1,8192]{2,1,0:T(1,128)S(1)} %bitcast.173), channel_id=1, replica_groups=mesh['clu'=32,'sub'=8] {'sub'}, dimensions={0}, use_global_device_ids=true | all-gather | bytes 294912 | tf_op jit(solution)/shard_map/all_gather | solution.py:60
  505.8 3.1 fusion.49
  510.1 2.5 copy.84
  514.7 7.0 %collective-permute-start.24 = (f32[128,3,128]{2,1,0:T(4,128)S(1)}, f32[128,3,128]{2,1,0:T(4,128)S(1)}, u32[]{:S(2)}, u32[]{:S(2)}) collective-permute-start(f32[128,3,128]{2,1,0:T(4,128)S(1)} %get-tuple-element.14), channel_id=1, source_target_pairs={{0,8},{8,0},{16,24},{24,16},{32,40},{40,32},{48,56},{56,48},{64,72... | collective-permute-start | bytes 589832 | tf_op jit(solution)/shard_map/ppermute | solution.py:16
  525.5 4.0 collective-permute-done.27
  531.5 5.0 collective-permute-done.25
  539.4 2.4 copy.86
  546.2 18.4 %all-gather.6 = f32[8,1,8192]{2,1,0:T(1,128)S(1)} all-gather(f32[1,1,8192]{2,1,0:T(1,128)S(1)} %bitcast.174), channel_id=1, replica_groups=mesh['clu'=32,'sub'=8] {'sub'}, dimensions={0}, use_global_device_ids=true | all-gather | bytes 294912 | tf_op jit(solution)/shard_map/all_gather | solution.py:60
  567.7 78.6 %all-reduce = (f32[128]{0:T(128)}, f32[128]{0:T(128)}) all-reduce(f32[128]{0:T(128)S(1)} %get-tuple-element.3, f32[128]{0:T(128)S(1)} %get-tuple-element.2), channel_id=1, replica_groups=mesh['clu'=32,'sub'=8] {'clu','sub'}, use_global_device_ids=true, to_apply=%region_9.0 | all-reduce | flops 256 | bytes 2048 | tf_op jit(solution)/shard_map/psum | solution.py:76
  647.0 2.9 multiply_subtract_fusion
  (155 shorter events, 133.0 us)
Async XLA Ops:
  0.6 27.7 %copy-start = (f32[64,1536]{1,0:T(8,128)S(1)}, f32[64,1536]{1,0:T(8,128)}, u32[]{:S(2)}) copy-start(f32[64,1536]{1,0:T(8,128)} %param.13) | copy-start | bytes 1179652
  0.6 4.2 copy-start.4
  4.1 8.2 %copy-start.5 = (s32[8]{0:T(128)S(1)}, s32[8]{0:T(128)}, u32[]{:S(2)}) copy-start(s32[8]{0:T(128)} %param.17) | copy-start | bytes 100
  4.1 9.4 %copy-start.6 = (s32[1,4]{1,0:T(1,128)S(1)}, s32[1,4]{1,0:T(1,128)}, u32[]{:S(2)}) copy-start(s32[1,4]{1,0:T(1,128)} %param.16) | copy-start | bytes 52
  5.7 8.6 %collective-permute-start = (f32[128,3,128]{2,1,0:T(4,128)S(1)}, f32[128,3,128]{2,1,0:T(4,128)S(1)}, u32[]{:S(2)}, u32[]{:S(2)}) collective-permute-start(f32[128,3,128]{2,1,0:T(4,128)S(1)} %get-tuple-element.38), channel_id=1, source_target_pairs={{0,8},{8,0},{16,24},{24,16},{32,40},{40,32},{48,56},{56,48},{64,72... | collective-permute-start | bytes 589832 | tf_op jit(solution)/shard_map/ppermute | solution.py:16
  9.0 7.8 %collective-permute-start.3 = (f32[128,3,128]{2,1,0:T(4,128)S(1)}, f32[128,3,128]{2,1,0:T(4,128)S(1)}, u32[]{:S(2)}, u32[]{:S(2)}) collective-permute-start(f32[128,3,128]{2,1,0:T(4,128)S(1)} %get-tuple-element.39), channel_id=1, source_target_pairs={{0,1},{1,0},{2,3},{3,2},{4,5},{5,4},{6,7},{7,6},{8,9},{9,8},{10,11... | collective-permute-start | bytes 589832 | tf_op jit(solution)/shard_map/ppermute | solution.py:16
  9.0 9.1 %collective-permute-start.2 = (f32[128,3,128]{2,1,0:T(4,128)S(1)}, f32[128,3,128]{2,1,0:T(4,128)S(1)}, u32[]{:S(2)}, u32[]{:S(2)}) collective-permute-start(f32[128,3,128]{2,1,0:T(4,128)S(1)} %get-tuple-element.40), channel_id=1, source_target_pairs={{0,32},{8,40},{16,48},{24,56},{32,0},{40,8},{48,16},{56,24},{64,96... | collective-permute-start | bytes 589832 | tf_op jit(solution)/shard_map/ppermute | solution.py:16
  11.8 12.0 %collective-permute-start.1 = (f32[128,3,128]{2,1,0:T(4,128)S(1)}, f32[128,3,128]{2,1,0:T(4,128)S(1)}, u32[]{:S(2)}, u32[]{:S(2)}) collective-permute-start(f32[128,3,128]{2,1,0:T(4,128)S(1)} %get-tuple-element.41), channel_id=1, source_target_pairs={{0,16},{8,24},{16,0},{24,8},{32,48},{40,56},{48,32},{56,40},{64,80... | collective-permute-start | bytes 589832 | tf_op jit(solution)/shard_map/ppermute | solution.py:16
  18.1 34.3 %copy-start.3 = (f32[64,512]{1,0:T(8,128)S(1)}, f32[64,512]{1,0:T(8,128)}, u32[]{:S(2)}) copy-start(f32[64,512]{1,0:T(8,128)} %param.14) | copy-start | bytes 393220
  61.6 9.5 %collective-permute-start.4 = (f32[128,3,128]{2,1,0:T(4,128)S(1)}, f32[128,3,128]{2,1,0:T(4,128)S(1)}, u32[]{:S(2)}, u32[]{:S(2)}) collective-permute-start(f32[128,3,128]{2,1,0:T(4,128)S(1)} %get-tuple-element.34), channel_id=1, source_target_pairs={{0,8},{8,0},{16,24},{24,16},{32,40},{40,32},{48,56},{56,48},{64,72... | collective-permute-start | bytes 589832 | tf_op jit(solution)/shard_map/ppermute | solution.py:16
  68.6 7.8 %collective-permute-start.7 = (f32[128,3,128]{2,1,0:T(4,128)S(1)}, f32[128,3,128]{2,1,0:T(4,128)S(1)}, u32[]{:S(2)}, u32[]{:S(2)}) collective-permute-start(f32[128,3,128]{2,1,0:T(4,128)S(1)} %get-tuple-element.35), channel_id=1, source_target_pairs={{0,1},{1,0},{2,3},{3,2},{4,5},{5,4},{6,7},{7,6},{8,9},{9,8},{10,11... | collective-permute-start | bytes 589832 | tf_op jit(solution)/shard_map/ppermute | solution.py:16
  69.4 9.0 %collective-permute-start.6 = (f32[128,3,128]{2,1,0:T(4,128)S(1)}, f32[128,3,128]{2,1,0:T(4,128)S(1)}, u32[]{:S(2)}, u32[]{:S(2)}) collective-permute-start(f32[128,3,128]{2,1,0:T(4,128)S(1)} %get-tuple-element.36), channel_id=1, source_target_pairs={{0,32},{8,40},{16,48},{24,56},{32,0},{40,8},{48,16},{56,24},{64,96... | collective-permute-start | bytes 589832 | tf_op jit(solution)/shard_map/ppermute | solution.py:16
  71.0 11.4 %collective-permute-start.5 = (f32[128,3,128]{2,1,0:T(4,128)S(1)}, f32[128,3,128]{2,1,0:T(4,128)S(1)}, u32[]{:S(2)}, u32[]{:S(2)}) collective-permute-start(f32[128,3,128]{2,1,0:T(4,128)S(1)} %get-tuple-element.37), channel_id=1, source_target_pairs={{0,16},{8,24},{16,0},{24,8},{32,48},{40,56},{48,32},{56,40},{64,80... | collective-permute-start | bytes 589832 | tf_op jit(solution)/shard_map/ppermute | solution.py:16
  119.2 10.4 %collective-permute-start.8 = (f32[128,3,128]{2,1,0:T(4,128)S(1)}, f32[128,3,128]{2,1,0:T(4,128)S(1)}, u32[]{:S(2)}, u32[]{:S(2)}) collective-permute-start(f32[128,3,128]{2,1,0:T(4,128)S(1)} %get-tuple-element.30), channel_id=1, source_target_pairs={{0,8},{8,0},{16,24},{24,16},{32,40},{40,32},{48,56},{56,48},{64,72... | collective-permute-start | bytes 589832 | tf_op jit(solution)/shard_map/ppermute | solution.py:16
  126.1 7.8 %collective-permute-start.11 = (f32[128,3,128]{2,1,0:T(4,128)S(1)}, f32[128,3,128]{2,1,0:T(4,128)S(1)}, u32[]{:S(2)}, u32[]{:S(2)}) collective-permute-start(f32[128,3,128]{2,1,0:T(4,128)S(1)} %get-tuple-element.31), channel_id=1, source_target_pairs={{0,1},{1,0},{2,3},{3,2},{4,5},{5,4},{6,7},{7,6},{8,9},{9,8},{10,11... | collective-permute-start | bytes 589832 | tf_op jit(solution)/shard_map/ppermute | solution.py:16
  126.1 9.8 %collective-permute-start.10 = (f32[128,3,128]{2,1,0:T(4,128)S(1)}, f32[128,3,128]{2,1,0:T(4,128)S(1)}, u32[]{:S(2)}, u32[]{:S(2)}) collective-permute-start(f32[128,3,128]{2,1,0:T(4,128)S(1)} %get-tuple-element.32), channel_id=1, source_target_pairs={{0,32},{8,40},{16,48},{24,56},{32,0},{40,8},{48,16},{56,24},{64,96... | collective-permute-start | bytes 589832 | tf_op jit(solution)/shard_map/ppermute | solution.py:16
  129.5 10.9 %collective-permute-start.9 = (f32[128,3,128]{2,1,0:T(4,128)S(1)}, f32[128,3,128]{2,1,0:T(4,128)S(1)}, u32[]{:S(2)}, u32[]{:S(2)}) collective-permute-start(f32[128,3,128]{2,1,0:T(4,128)S(1)} %get-tuple-element.33), channel_id=1, source_target_pairs={{0,16},{8,24},{16,0},{24,8},{32,48},{40,56},{48,32},{56,40},{64,80... | collective-permute-start | bytes 589832 | tf_op jit(solution)/shard_map/ppermute | solution.py:16
  262.2 4.4 collective-permute-start.12
  263.0 7.8 %collective-permute-start.15 = (f32[128,3,128]{2,1,0:T(4,128)S(1)}, f32[128,3,128]{2,1,0:T(4,128)S(1)}, u32[]{:S(2)}, u32[]{:S(2)}) collective-permute-start(f32[128,3,128]{2,1,0:T(4,128)S(1)} %get-tuple-element.27), channel_id=1, source_target_pairs={{0,1},{1,0},{2,3},{3,2},{4,5},{5,4},{6,7},{7,6},{8,9},{9,8},{10,11... | collective-permute-start | bytes 589832 | tf_op jit(solution)/shard_map/ppermute | solution.py:16
  264.2 9.0 %collective-permute-start.14 = (f32[128,3,128]{2,1,0:T(4,128)S(1)}, f32[128,3,128]{2,1,0:T(4,128)S(1)}, u32[]{:S(2)}, u32[]{:S(2)}) collective-permute-start(f32[128,3,128]{2,1,0:T(4,128)S(1)} %get-tuple-element.28), channel_id=1, source_target_pairs={{0,32},{8,40},{16,48},{24,56},{32,0},{40,8},{48,16},{56,24},{64,96... | collective-permute-start | bytes 589832 | tf_op jit(solution)/shard_map/ppermute | solution.py:16
  265.3 12.9 %collective-permute-start.13 = (f32[128,3,128]{2,1,0:T(4,128)S(1)}, f32[128,3,128]{2,1,0:T(4,128)S(1)}, u32[]{:S(2)}, u32[]{:S(2)}) collective-permute-start(f32[128,3,128]{2,1,0:T(4,128)S(1)} %get-tuple-element.29), channel_id=1, source_target_pairs={{0,16},{8,24},{16,0},{24,8},{32,48},{40,56},{48,32},{56,40},{64,80... | collective-permute-start | bytes 589832 | tf_op jit(solution)/shard_map/ppermute | solution.py:16
  317.1 9.1 %collective-permute-start.16 = (f32[128,3,128]{2,1,0:T(4,128)S(1)}, f32[128,3,128]{2,1,0:T(4,128)S(1)}, u32[]{:S(2)}, u32[]{:S(2)}) collective-permute-start(f32[128,3,128]{2,1,0:T(4,128)S(1)} %get-tuple-element.22), channel_id=1, source_target_pairs={{0,8},{8,0},{16,24},{24,16},{32,40},{40,32},{48,56},{56,48},{64,72... | collective-permute-start | bytes 589832 | tf_op jit(solution)/shard_map/ppermute | solution.py:16
  324.1 7.8 %collective-permute-start.19 = (f32[128,3,128]{2,1,0:T(4,128)S(1)}, f32[128,3,128]{2,1,0:T(4,128)S(1)}, u32[]{:S(2)}, u32[]{:S(2)}) collective-permute-start(f32[128,3,128]{2,1,0:T(4,128)S(1)} %get-tuple-element.23), channel_id=1, source_target_pairs={{0,1},{1,0},{2,3},{3,2},{4,5},{5,4},{6,7},{7,6},{8,9},{9,8},{10,11... | collective-permute-start | bytes 589832 | tf_op jit(solution)/shard_map/ppermute | solution.py:16
  324.1 9.2 %collective-permute-start.18 = (f32[128,3,128]{2,1,0:T(4,128)S(1)}, f32[128,3,128]{2,1,0:T(4,128)S(1)}, u32[]{:S(2)}, u32[]{:S(2)}) collective-permute-start(f32[128,3,128]{2,1,0:T(4,128)S(1)} %get-tuple-element.24), channel_id=1, source_target_pairs={{0,32},{8,40},{16,48},{24,56},{32,0},{40,8},{48,16},{56,24},{64,96... | collective-permute-start | bytes 589832 | tf_op jit(solution)/shard_map/ppermute | solution.py:16
  325.9 11.6 %collective-permute-start.17 = (f32[128,3,128]{2,1,0:T(4,128)S(1)}, f32[128,3,128]{2,1,0:T(4,128)S(1)}, u32[]{:S(2)}, u32[]{:S(2)}) collective-permute-start(f32[128,3,128]{2,1,0:T(4,128)S(1)} %get-tuple-element.25), channel_id=1, source_target_pairs={{0,16},{8,24},{16,0},{24,8},{32,48},{40,56},{48,32},{56,40},{64,80... | collective-permute-start | bytes 589832 | tf_op jit(solution)/shard_map/ppermute | solution.py:16
  459.1 3.1 collective-permute-start.20
  460.1 7.8 %collective-permute-start.23 = (f32[128,3,128]{2,1,0:T(4,128)S(1)}, f32[128,3,128]{2,1,0:T(4,128)S(1)}, u32[]{:S(2)}, u32[]{:S(2)}) collective-permute-start(f32[128,3,128]{2,1,0:T(4,128)S(1)} %get-tuple-element.19), channel_id=1, source_target_pairs={{0,1},{1,0},{2,3},{3,2},{4,5},{5,4},{6,7},{7,6},{8,9},{9,8},{10,11... | collective-permute-start | bytes 589832 | tf_op jit(solution)/shard_map/ppermute | solution.py:16
  461.4 9.0 %collective-permute-start.22 = (f32[128,3,128]{2,1,0:T(4,128)S(1)}, f32[128,3,128]{2,1,0:T(4,128)S(1)}, u32[]{:S(2)}, u32[]{:S(2)}) collective-permute-start(f32[128,3,128]{2,1,0:T(4,128)S(1)} %get-tuple-element.20), channel_id=1, source_target_pairs={{0,32},{8,40},{16,48},{24,56},{32,0},{40,8},{48,16},{56,24},{64,96... | collective-permute-start | bytes 589832 | tf_op jit(solution)/shard_map/ppermute | solution.py:16
  462.3 11.5 %collective-permute-start.21 = (f32[128,3,128]{2,1,0:T(4,128)S(1)}, f32[128,3,128]{2,1,0:T(4,128)S(1)}, u32[]{:S(2)}, u32[]{:S(2)}) collective-permute-start(f32[128,3,128]{2,1,0:T(4,128)S(1)} %get-tuple-element.21), channel_id=1, source_target_pairs={{0,16},{8,24},{16,0},{24,8},{32,48},{40,56},{48,32},{56,40},{64,80... | collective-permute-start | bytes 589832 | tf_op jit(solution)/shard_map/ppermute | solution.py:16
  504.9 0.9 copy-start.1
  514.7 10.0 %collective-permute-start.24 = (f32[128,3,128]{2,1,0:T(4,128)S(1)}, f32[128,3,128]{2,1,0:T(4,128)S(1)}, u32[]{:S(2)}, u32[]{:S(2)}) collective-permute-start(f32[128,3,128]{2,1,0:T(4,128)S(1)} %get-tuple-element.14), channel_id=1, source_target_pairs={{0,8},{8,0},{16,24},{24,16},{32,40},{40,32},{48,56},{56,48},{64,72... | collective-permute-start | bytes 589832 | tf_op jit(solution)/shard_map/ppermute | solution.py:16
  521.7 7.8 %collective-permute-start.27 = (f32[128,3,128]{2,1,0:T(4,128)S(1)}, f32[128,3,128]{2,1,0:T(4,128)S(1)}, u32[]{:S(2)}, u32[]{:S(2)}) collective-permute-start(f32[128,3,128]{2,1,0:T(4,128)S(1)} %get-tuple-element.15), channel_id=1, source_target_pairs={{0,1},{1,0},{2,3},{3,2},{4,5},{5,4},{6,7},{7,6},{8,9},{9,8},{10,11... | collective-permute-start | bytes 589832 | tf_op jit(solution)/shard_map/ppermute | solution.py:16
  521.7 9.2 %collective-permute-start.26 = (f32[128,3,128]{2,1,0:T(4,128)S(1)}, f32[128,3,128]{2,1,0:T(4,128)S(1)}, u32[]{:S(2)}, u32[]{:S(2)}) collective-permute-start(f32[128,3,128]{2,1,0:T(4,128)S(1)} %get-tuple-element.16), channel_id=1, source_target_pairs={{0,32},{8,40},{16,48},{24,56},{32,0},{40,8},{48,16},{56,24},{64,96... | collective-permute-start | bytes 589832 | tf_op jit(solution)/shard_map/ppermute | solution.py:16
  523.4 13.2 %collective-permute-start.25 = (f32[128,3,128]{2,1,0:T(4,128)S(1)}, f32[128,3,128]{2,1,0:T(4,128)S(1)}, u32[]{:S(2)}, u32[]{:S(2)}) collective-permute-start(f32[128,3,128]{2,1,0:T(4,128)S(1)} %get-tuple-element.17), channel_id=1, source_target_pairs={{0,16},{8,24},{16,0},{24,8},{32,48},{40,56},{48,32},{56,40},{64,80... | collective-permute-start | bytes 589832 | tf_op jit(solution)/shard_map/ppermute | solution.py:16
  545.3 101.8 %copy-start.2 = (f32[128,1536]{1,0:T(8,128)S(1)}, f32[128,1536]{1,0:T(8,128)}, u32[]{:S(2)}) copy-start(f32[128,1536]{1,0:T(8,128)} %copy-done.1) | copy-start | bytes 2359300
where the time goes:
time: 661 us; the launch traced here: 650 us
  blocking collectives  375 us (57%)
  matrix products  70.3 us (11%)
  waiting for transfers between devices  63.1 us (10%)
  starting transfers between devices  53 us (8%)
  local copies, waits for them, and re-layouts  52.9 us (8%)
  other arithmetic  33.6 us (5%)
    psum x3, blocking collectives, on_device(): cross_all, image_all = lax.psum((cross_sum, image_sum), ('clu', 'sub'))  240 us
    all_gather x7, blocking collectives, coarse(): piece = lax.all_gather(flat, 'sub', axis=0, tiled=True)  135 us
    ppermute x28, waiting for transfers between devices, from_partner(): return lax.ppermute(value, axis, pairs)  63.1 us
    ppermute x28, starting transfers between devices, from_partner(): return lax.ppermute(value, axis, pairs)  53 us
    dot_general x7, matrix products, apply_local(): jnp.dot(vector.astype(jnp.bfloat16), matrix, preferred_element_type=jnp.f...  22.2 us
    mul x21, other arithmetic, assemble(): received.append(incoming * edge_gates[colour])  14.8 us
    transpose x7, local copies, waits for them, and re-layouts, assemble(): added = jnp.einsum('jq,kjb->kqb', onehot, joined, precision=HIGH)  14.7 us
    reshape x7, local copies, waits for them, and re-layouts, assemble(): blocked = product.reshape(cases, blocks, BLK)  14.5 us
  transfers between devices with their start and end apart: 28, of which 21 were waited for; matrix products, arithmetic and copies ran while one was open for 3% of the time, Pallas kernels for 0%

commit v1 on v0

--- a/solution.py
+++ b/solution.py
@@ -8,6 +8,11 @@
 NCOL = 4
 ITERS = 3
 HIGH = lax.Precision.HIGHEST
+
+
+def one_after_other(array, one, other):
+    partial = lax.psum(array, one)
+    return lax.psum(partial, other)
 
 
 def from_partner(value, axis, bit):
@@ -73,7 +78,7 @@
         image = coarse(assemble(apply_local(search, dual_blocks)))
         cross_sum = jnp.sum(residual * image, axis=1)
         image_sum = jnp.sum(image * image, axis=1)
-        cross_all, image_all = lax.psum((cross_sum, image_sum), ("clu", "sub"))
+        cross_all, image_all = one_after_other((cross_sum, image_sum), "clu", "sub")
         step_len = cross_all / (image_all + 1e-06)
         multipliers = multipliers + step_len[:, None] * search
         residual = residual - step_len[:, None] * image

time: 661 us -> 672 us (1.017)
    psum x3 -> x6, blocking collectives: 240 us -> 246 us  [the longest x3 209 us: one_after_other(): partial = lax.psum(array, one)]
  transfers between devices with their start and end apart: 28 -> 28, of which waited for: 21 -> 23; matrix products, arithmetic and copies ran while one was open for 3% -> 2% of each run, Pallas kernels for 0% -> 0%
where the time goes in v1:
time: 672 us; the launch traced here: 660 us
  blocking collectives  381 us (57%)
  matrix products  70.3 us (10%)
  waiting for transfers between devices  63.3 us (9%)
  starting transfers between devices  58.8 us (9%)
  local copies, waits for them, and re-layouts  52.9 us (8%)
  other arithmetic  32.3 us (5%)
    psum x3, blocking collectives, one_after_other(): partial = lax.psum(array, one)  209 us
    all_gather x7, blocking collectives, coarse(): piece = lax.all_gather(flat, 'sub', axis=0, tiled=True)  135 us
    ppermute x28, waiting for transfers between devices, from_partner(): return lax.ppermute(value, axis, pairs)  63.3 us
    ppermute x28, starting transfers between devices, from_partner(): return lax.ppermute(value, axis, pairs)  58.8 us
    psum x3, blocking collectives, one_after_other(): return lax.psum(partial, other)  36.9 us
    dot_general x7, matrix products, apply_local(): jnp.dot(vector.astype(jnp.bfloat16), matrix, preferred_element_type=jnp.f...  22.2 us
    transpose x7, local copies, waits for them, and re-layouts, assemble(): added = jnp.einsum('jq,kjb->kqb', onehot, joined, precision=HIGH)  14.7 us
    reshape x7, local copies, waits for them, and re-layouts, assemble(): blocked = product.reshape(cases, blocks, BLK)  14.5 us
  transfers between devices with their start and end apart: 28, of which 23 were waited for; matrix products, arithmetic and copies ran while one was open for 2% of the time, Pallas kernels for 0%

profile of v1, /device:TPU:1, one launch (start us, length us, event | category | flops | bytes accessed | tf_op | source)
XLA Modules:
  0.0 660.2 jit_solution(7384560515012006873)
XLA Ops:
  0.7 3.4 fusion.61
  5.7 3.3 collective-permute-start
  9.0 2.8 collective-permute-start.2
  18.8 5.1 collective-permute-done.1
  30.3 21.9 %all-gather = f32[8,1,8192]{2,1,0:T(1,128)S(1)} all-gather(f32[1,1,8192]{2,1,0:T(1,128)S(1)} %bitcast.168), channel_id=1, replica_groups=mesh['clu'=32,'sub'=8] {'sub'}, dimensions={0}, use_global_device_ids=true | all-gather | bytes 294912 | tf_op jit(solution)/shard_map/all_gather | solution.py:65
  54.7 3.1 fusion.59
  61.6 7.0 %collective-permute-start.4 = (f32[128,3,128]{2,1,0:T(4,128)S(1)}, f32[128,3,128]{2,1,0:T(4,128)S(1)}, u32[]{:S(2)}, u32[]{:S(2)}) collective-permute-start(f32[128,3,128]{2,1,0:T(4,128)S(1)} %get-tuple-element.40), channel_id=1, source_target_pairs={{0,8},{8,0},{16,24},{24,16},{32,40},{40,32},{48,56},{56,48},{64,72... | collective-permute-start | bytes 589832 | tf_op jit(solution)/shard_map/ppermute | solution.py:21
  71.7 4.6 collective-permute-done.7
  79.0 3.3 collective-permute-done.5
  89.9 19.1 %all-gather.1 = f32[8,1,8192]{2,1,0:T(1,128)S(1)} all-gather(f32[1,1,8192]{2,1,0:T(1,128)S(1)} %bitcast.169), channel_id=1, replica_groups=mesh['clu'=32,'sub'=8] {'sub'}, dimensions={0}, use_global_device_ids=true | all-gather | bytes 294912 | tf_op jit(solution)/shard_map/all_gather | solution.py:65
  110.2 3.1 fusion.57
  114.5 2.5 copy.64
  119.0 6.9 %collective-permute-start.8 = (f32[128,3,128]{2,1,0:T(4,128)S(1)}, f32[128,3,128]{2,1,0:T(4,128)S(1)}, u32[]{:S(2)}, u32[]{:S(2)}) collective-permute-start(f32[128,3,128]{2,1,0:T(4,128)S(1)} %get-tuple-element.36), channel_id=1, source_target_pairs={{0,8},{8,0},{16,24},{24,16},{32,40},{40,32},{48,56},{56,48},{64,72... | collective-permute-start | bytes 589832 | tf_op jit(solution)/shard_map/ppermute | solution.py:21
  125.9 3.5 collective-permute-start.10
  130.1 3.6 collective-permute-done.11
  136.4 3.9 collective-permute-done.9
  143.1 2.4 copy.66
  149.9 18.5 %all-gather.2 = f32[8,1,8192]{2,1,0:T(1,128)S(1)} all-gather(f32[1,1,8192]{2,1,0:T(1,128)S(1)} %bitcast.170), channel_id=1, replica_groups=mesh['clu'=32,'sub'=8] {'sub'}, dimensions={0}, use_global_device_ids=true | all-gather | bytes 294912 | tf_op jit(solution)/shard_map/all_gather | solution.py:65
  170.6 69.5 %all-reduce.2 = (f32[128]{0:T(128)S(1)}, f32[128]{0:T(128)S(1)}) all-reduce(f32[128]{0:T(128)S(1)} %get-tuple-element.7, f32[128]{0:T(128)S(1)} %get-tuple-element.6), channel_id=1, replica_groups=mesh['clu'=32,'sub'=8] {'clu'}, use_global_device_ids=true, to_apply=%region_1.0 | all-reduce | flops 256 | bytes 2048 | tf_op jit(solution)/shard_map/psum | solution.py:14
  240.1 12.3 %all-reduce.5 = (f32[128]{0:T(128)S(1)}, f32[128]{0:T(128)S(1)}) all-reduce(f32[128]{0:T(128)S(1)} %get-tuple-element.12, f32[128]{0:T(128)S(1)} %get-tuple-element.13), channel_id=1, replica_groups=mesh['clu'=32,'sub'=8] {'sub'}, use_global_device_ids=true, to_apply=%region_2.0 | all-reduce | flops 256 | bytes 2048 | tf_op jit(solution)/shard_map/psum | solution.py:15
  253.7 3.1 fusion.55
  257.9 2.5 copy.69
  262.5 4.5 collective-permute-start.12
  268.8 5.9 collective-permute-done.15
  287.8 19.1 %all-gather.3 = f32[8,1,8192]{2,1,0:T(1,128)S(1)} all-gather(f32[1,1,8192]{2,1,0:T(1,128)S(1)} %bitcast.171), channel_id=1, replica_groups=mesh['clu'=32,'sub'=8] {'sub'}, dimensions={0}, use_global_device_ids=true | all-gather | bytes 294912 | tf_op jit(solution)/shard_map/all_gather | solution.py:65
  308.1 3.1 fusion.53
  312.4 2.5 copy.74
  316.9 6.9 %collective-permute-start.16 = (f32[128,3,128]{2,1,0:T(4,128)S(1)}, f32[128,3,128]{2,1,0:T(4,128)S(1)}, u32[]{:S(2)}, u32[]{:S(2)}) collective-permute-start(f32[128,3,128]{2,1,0:T(4,128)S(1)} %get-tuple-element.28), channel_id=1, source_target_pairs={{0,8},{8,0},{16,24},{24,16},{32,40},{40,32},{48,56},{56,48},{64,72... | collective-permute-start | bytes 589832 | tf_op jit(solution)/shard_map/ppermute | solution.py:21
  324.1 2.7 collective-permute-start.18
  333.8 6.3 collective-permute-done.17
  349.7 18.5 %all-gather.4 = f32[8,1,8192]{2,1,0:T(1,128)S(1)} all-gather(f32[1,1,8192]{2,1,0:T(1,128)S(1)} %bitcast.172), channel_id=1, replica_groups=mesh['clu'=32,'sub'=8] {'sub'}, dimensions={0}, use_global_device_ids=true | all-gather | bytes 294912 | tf_op jit(solution)/shard_map/all_gather | solution.py:65
  371.2 69.5 %all-reduce.1 = (f32[128]{0:T(128)S(1)}, f32[128]{0:T(128)S(1)}) all-reduce(f32[128]{0:T(128)S(1)} %get-tuple-element.5, f32[128]{0:T(128)S(1)} %get-tuple-element.4), channel_id=1, replica_groups=mesh['clu'=32,'sub'=8] {'clu'}, use_global_device_ids=true, to_apply=%region_7.0 | all-reduce | flops 256 | bytes 2048 | tf_op jit(solution)/shard_map/psum | solution.py:14
  440.8 11.9 %all-reduce.4 = (f32[128]{0:T(128)S(1)}, f32[128]{0:T(128)S(1)}) all-reduce(f32[128]{0:T(128)S(1)} %get-tuple-element.10, f32[128]{0:T(128)S(1)} %get-tuple-element.11), channel_id=1, replica_groups=mesh['clu'=32,'sub'=8] {'sub'}, use_global_device_ids=true, to_apply=%region_8.0 | all-reduce | flops 256 | bytes 2048 | tf_op jit(solution)/shard_map/psum | solution.py:15
  454.0 3.1 fusion.51
  458.3 2.5 copy.79
  462.8 4.5 collective-permute-start.20
  469.2 5.9 collective-permute-done.23
  488.3 19.3 %all-gather.5 = f32[8,1,8192]{2,1,0:T(1,128)S(1)} all-gather(f32[1,1,8192]{2,1,0:T(1,128)S(1)} %bitcast.173), channel_id=1, replica_groups=mesh['clu'=32,'sub'=8] {'sub'}, dimensions={0}, use_global_device_ids=true | all-gather | bytes 294912 | tf_op jit(solution)/shard_map/all_gather | solution.py:65
  510.7 3.1 fusion.49
  514.9 2.5 copy.84
  519.5 6.9 %collective-permute-start.24 = (f32[128,3,128]{2,1,0:T(4,128)S(1)}, f32[128,3,128]{2,1,0:T(4,128)S(1)}, u32[]{:S(2)}, u32[]{:S(2)}) collective-permute-start(f32[128,3,128]{2,1,0:T(4,128)S(1)} %get-tuple-element.20), channel_id=1, source_target_pairs={{0,8},{8,0},{16,24},{24,16},{32,40},{40,32},{48,56},{56,48},{64,72... | collective-permute-start | bytes 589832 | tf_op jit(solution)/shard_map/ppermute | solution.py:21
  526.4 2.8 collective-permute-start.26
  531.5 2.7 collective-permute-done.27
  536.1 6.3 collective-permute-done.25
  552.0 18.5 %all-gather.6 = f32[8,1,8192]{2,1,0:T(1,128)S(1)} all-gather(f32[1,1,8192]{2,1,0:T(1,128)S(1)} %bitcast.174), channel_id=1, replica_groups=mesh['clu'=32,'sub'=8] {'sub'}, dimensions={0}, use_global_device_ids=true | all-gather | bytes 294912 | tf_op jit(solution)/shard_map/all_gather | solution.py:65
  573.6 70.0 %all-reduce = (f32[128]{0:T(128)}, f32[128]{0:T(128)}) all-reduce(f32[128]{0:T(128)S(1)} %get-tuple-element.3, f32[128]{0:T(128)S(1)} %get-tuple-element.2), channel_id=1, replica_groups=mesh['clu'=32,'sub'=8] {'clu'}, use_global_device_ids=true, to_apply=%region_13.0 | all-reduce | flops 256 | bytes 2048 | tf_op jit(solution)/shard_map/psum | solution.py:14
  643.7 12.7 %all-reduce.3 = (f32[128]{0:T(128)S(1)}, f32[128]{0:T(128)}) all-reduce(f32[128]{0:T(128)} %get-tuple-element.8, f32[128]{0:T(128)} %get-tuple-element.9), channel_id=1, replica_groups=mesh['clu'=32,'sub'=8] {'sub'}, use_global_device_ids=true, to_apply=%region_14.0 | all-reduce | flops 256 | bytes 2048 | tf_op jit(solution)/shard_map/psum | solution.py:15
  657.1 2.9 multiply_subtract_fusion
  (158 shorter events, 138.1 us)
Async XLA Ops:
  0.6 27.6 %copy-start = (f32[64,1536]{1,0:T(8,128)S(1)}, f32[64,1536]{1,0:T(8,128)}, u32[]{:S(2)}) copy-start(f32[64,1536]{1,0:T(8,128)} %param.13) | copy-start | bytes 1179652
  0.6 4.2 copy-start.4
  4.1 8.2 %copy-start.5 = (s32[8]{0:T(128)S(1)}, s32[8]{0:T(128)}, u32[]{:S(2)}) copy-start(s32[8]{0:T(128)} %param.17) | copy-start | bytes 100
  4.1 9.4 %copy-start.6 = (s32[1,4]{1,0:T(1,128)S(1)}, s32[1,4]{1,0:T(1,128)}, u32[]{:S(2)}) copy-start(s32[1,4]{1,0:T(1,128)} %param.16) | copy-start | bytes 52
  5.7 8.6 %collective-permute-start = (f32[128,3,128]{2,1,0:T(4,128)S(1)}, f32[128,3,128]{2,1,0:T(4,128)S(1)}, u32[]{:S(2)}, u32[]{:S(2)}) collective-permute-start(f32[128,3,128]{2,1,0:T(4,128)S(1)} %get-tuple-element.44), channel_id=1, source_target_pairs={{0,8},{8,0},{16,24},{24,16},{32,40},{40,32},{48,56},{56,48},{64,72... | collective-permute-start | bytes 589832 | tf_op jit(solution)/shard_map/ppermute | solution.py:21
  9.0 7.8 %collective-permute-start.3 = (f32[128,3,128]{2,1,0:T(4,128)S(1)}, f32[128,3,128]{2,1,0:T(4,128)S(1)}, u32[]{:S(2)}, u32[]{:S(2)}) collective-permute-start(f32[128,3,128]{2,1,0:T(4,128)S(1)} %get-tuple-element.45), channel_id=1, source_target_pairs={{0,1},{1,0},{2,3},{3,2},{4,5},{5,4},{6,7},{7,6},{8,9},{9,8},{10,11... | collective-permute-start | bytes 589832 | tf_op jit(solution)/shard_map/ppermute | solution.py:21
  9.0 9.1 %collective-permute-start.2 = (f32[128,3,128]{2,1,0:T(4,128)S(1)}, f32[128,3,128]{2,1,0:T(4,128)S(1)}, u32[]{:S(2)}, u32[]{:S(2)}) collective-permute-start(f32[128,3,128]{2,1,0:T(4,128)S(1)} %get-tuple-element.46), channel_id=1, source_target_pairs={{0,32},{8,40},{16,48},{24,56},{32,0},{40,8},{48,16},{56,24},{64,96... | collective-permute-start | bytes 589832 | tf_op jit(solution)/shard_map/ppermute | solution.py:21
  11.8 12.0 %collective-permute-start.1 = (f32[128,3,128]{2,1,0:T(4,128)S(1)}, f32[128,3,128]{2,1,0:T(4,128)S(1)}, u32[]{:S(2)}, u32[]{:S(2)}) collective-permute-start(f32[128,3,128]{2,1,0:T(4,128)S(1)} %get-tuple-element.47), channel_id=1, source_target_pairs={{0,16},{8,24},{16,0},{24,8},{32,48},{40,56},{48,32},{56,40},{64,80... | collective-permute-start | bytes 589832 | tf_op jit(solution)/shard_map/ppermute | solution.py:21
  18.1 34.2 %copy-start.3 = (f32[64,512]{1,0:T(8,128)S(1)}, f32[64,512]{1,0:T(8,128)}, u32[]{:S(2)}) copy-start(f32[64,512]{1,0:T(8,128)} %param.14) | copy-start | bytes 393220
  61.6 9.5 %collective-permute-start.4 = (f32[128,3,128]{2,1,0:T(4,128)S(1)}, f32[128,3,128]{2,1,0:T(4,128)S(1)}, u32[]{:S(2)}, u32[]{:S(2)}) collective-permute-start(f32[128,3,128]{2,1,0:T(4,128)S(1)} %get-tuple-element.40), channel_id=1, source_target_pairs={{0,8},{8,0},{16,24},{24,16},{32,40},{40,32},{48,56},{56,48},{64,72... | collective-permute-start | bytes 589832 | tf_op jit(solution)/shard_map/ppermute | solution.py:21
  68.5 7.8 %collective-permute-start.7 = (f32[128,3,128]{2,1,0:T(4,128)S(1)}, f32[128,3,128]{2,1,0:T(4,128)S(1)}, u32[]{:S(2)}, u32[]{:S(2)}) collective-permute-start(f32[128,3,128]{2,1,0:T(4,128)S(1)} %get-tuple-element.41), channel_id=1, source_target_pairs={{0,1},{1,0},{2,3},{3,2},{4,5},{5,4},{6,7},{7,6},{8,9},{9,8},{10,11... | collective-permute-start | bytes 589832 | tf_op jit(solution)/shard_map/ppermute | solution.py:21
  69.3 9.0 %collective-permute-start.6 = (f32[128,3,128]{2,1,0:T(4,128)S(1)}, f32[128,3,128]{2,1,0:T(4,128)S(1)}, u32[]{:S(2)}, u32[]{:S(2)}) collective-permute-start(f32[128,3,128]{2,1,0:T(4,128)S(1)} %get-tuple-element.42), channel_id=1, source_target_pairs={{0,32},{8,40},{16,48},{24,56},{32,0},{40,8},{48,16},{56,24},{64,96... | collective-permute-start | bytes 589832 | tf_op jit(solution)/shard_map/ppermute | solution.py:21
  70.9 11.4 %collective-permute-start.5 = (f32[128,3,128]{2,1,0:T(4,128)S(1)}, f32[128,3,128]{2,1,0:T(4,128)S(1)}, u32[]{:S(2)}, u32[]{:S(2)}) collective-permute-start(f32[128,3,128]{2,1,0:T(4,128)S(1)} %get-tuple-element.43), channel_id=1, source_target_pairs={{0,16},{8,24},{16,0},{24,8},{32,48},{40,56},{48,32},{56,40},{64,80... | collective-permute-start | bytes 589832 | tf_op jit(solution)/shard_map/ppermute | solution.py:21
  119.0 10.4 %collective-permute-start.8 = (f32[128,3,128]{2,1,0:T(4,128)S(1)}, f32[128,3,128]{2,1,0:T(4,128)S(1)}, u32[]{:S(2)}, u32[]{:S(2)}) collective-permute-start(f32[128,3,128]{2,1,0:T(4,128)S(1)} %get-tuple-element.36), channel_id=1, source_target_pairs={{0,8},{8,0},{16,24},{24,16},{32,40},{40,32},{48,56},{56,48},{64,72... | collective-permute-start | bytes 589832 | tf_op jit(solution)/shard_map/ppermute | solution.py:21
  125.9 7.8 %collective-permute-start.11 = (f32[128,3,128]{2,1,0:T(4,128)S(1)}, f32[128,3,128]{2,1,0:T(4,128)S(1)}, u32[]{:S(2)}, u32[]{:S(2)}) collective-permute-start(f32[128,3,128]{2,1,0:T(4,128)S(1)} %get-tuple-element.37), channel_id=1, source_target_pairs={{0,1},{1,0},{2,3},{3,2},{4,5},{5,4},{6,7},{7,6},{8,9},{9,8},{10,11... | collective-permute-start | bytes 589832 | tf_op jit(solution)/shard_map/ppermute | solution.py:21
  125.9 9.8 %collective-permute-start.10 = (f32[128,3,128]{2,1,0:T(4,128)S(1)}, f32[128,3,128]{2,1,0:T(4,128)S(1)}, u32[]{:S(2)}, u32[]{:S(2)}) collective-permute-start(f32[128,3,128]{2,1,0:T(4,128)S(1)} %get-tuple-element.38), channel_id=1, source_target_pairs={{0,32},{8,40},{16,48},{24,56},{32,0},{40,8},{48,16},{56,24},{64,96... | collective-permute-start | bytes 589832 | tf_op jit(solution)/shard_map/ppermute | solution.py:21
  129.4 10.9 %collective-permute-start.9 = (f32[128,3,128]{2,1,0:T(4,128)S(1)}, f32[128,3,128]{2,1,0:T(4,128)S(1)}, u32[]{:S(2)}, u32[]{:S(2)}) collective-permute-start(f32[128,3,128]{2,1,0:T(4,128)S(1)} %get-tuple-element.39), channel_id=1, source_target_pairs={{0,16},{8,24},{16,0},{24,8},{32,48},{40,56},{48,32},{56,40},{64,80... | collective-permute-start | bytes 589832 | tf_op jit(solution)/shard_map/ppermute | solution.py:21
  262.5 5.7 collective-permute-start.12
  267.0 7.8 %collective-permute-start.15 = (f32[128,3,128]{2,1,0:T(4,128)S(1)}, f32[128,3,128]{2,1,0:T(4,128)S(1)}, u32[]{:S(2)}, u32[]{:S(2)}) collective-permute-start(f32[128,3,128]{2,1,0:T(4,128)S(1)} %get-tuple-element.33), channel_id=1, source_target_pairs={{0,1},{1,0},{2,3},{3,2},{4,5},{5,4},{6,7},{7,6},{8,9},{9,8},{10,11... | collective-permute-start | bytes 589832 | tf_op jit(solution)/shard_map/ppermute | solution.py:21
  267.0 9.0 %collective-permute-start.14 = (f32[128,3,128]{2,1,0:T(4,128)S(1)}, f32[128,3,128]{2,1,0:T(4,128)S(1)}, u32[]{:S(2)}, u32[]{:S(2)}) collective-permute-start(f32[128,3,128]{2,1,0:T(4,128)S(1)} %get-tuple-element.34), channel_id=1, source_target_pairs={{0,32},{8,40},{16,48},{24,56},{32,0},{40,8},{48,16},{56,24},{64,96... | collective-permute-start | bytes 589832 | tf_op jit(solution)/shard_map/ppermute | solution.py:21
  267.0 11.2 %collective-permute-start.13 = (f32[128,3,128]{2,1,0:T(4,128)S(1)}, f32[128,3,128]{2,1,0:T(4,128)S(1)}, u32[]{:S(2)}, u32[]{:S(2)}) collective-permute-start(f32[128,3,128]{2,1,0:T(4,128)S(1)} %get-tuple-element.35), channel_id=1, source_target_pairs={{0,16},{8,24},{16,0},{24,8},{32,48},{40,56},{48,32},{56,40},{64,80... | collective-permute-start | bytes 589832 | tf_op jit(solution)/shard_map/ppermute | solution.py:21
  316.9 11.9 %collective-permute-start.16 = (f32[128,3,128]{2,1,0:T(4,128)S(1)}, f32[128,3,128]{2,1,0:T(4,128)S(1)}, u32[]{:S(2)}, u32[]{:S(2)}) collective-permute-start(f32[128,3,128]{2,1,0:T(4,128)S(1)} %get-tuple-element.28), channel_id=1, source_target_pairs={{0,8},{8,0},{16,24},{24,16},{32,40},{40,32},{48,56},{56,48},{64,72... | collective-permute-start | bytes 589832 | tf_op jit(solution)/shard_map/ppermute | solution.py:21
  323.8 7.8 %collective-permute-start.19 = (f32[128,3,128]{2,1,0:T(4,128)S(1)}, f32[128,3,128]{2,1,0:T(4,128)S(1)}, u32[]{:S(2)}, u32[]{:S(2)}) collective-permute-start(f32[128,3,128]{2,1,0:T(4,128)S(1)} %get-tuple-element.29), channel_id=1, source_target_pairs={{0,1},{1,0},{2,3},{3,2},{4,5},{5,4},{6,7},{7,6},{8,9},{9,8},{10,11... | collective-permute-start | bytes 589832 | tf_op jit(solution)/shard_map/ppermute | solution.py:21
  324.1 9.0 %collective-permute-start.18 = (f32[128,3,128]{2,1,0:T(4,128)S(1)}, f32[128,3,128]{2,1,0:T(4,128)S(1)}, u32[]{:S(2)}, u32[]{:S(2)}) collective-permute-start(f32[128,3,128]{2,1,0:T(4,128)S(1)} %get-tuple-element.30), channel_id=1, source_target_pairs={{0,32},{8,40},{16,48},{24,56},{32,0},{40,8},{48,16},{56,24},{64,96... | collective-permute-start | bytes 589832 | tf_op jit(solution)/shard_map/ppermute | solution.py:21
  326.8 13.2 %collective-permute-start.17 = (f32[128,3,128]{2,1,0:T(4,128)S(1)}, f32[128,3,128]{2,1,0:T(4,128)S(1)}, u32[]{:S(2)}, u32[]{:S(2)}) collective-permute-start(f32[128,3,128]{2,1,0:T(4,128)S(1)} %get-tuple-element.31), channel_id=1, source_target_pairs={{0,16},{8,24},{16,0},{24,8},{32,48},{40,56},{48,32},{56,40},{64,80... | collective-permute-start | bytes 589832 | tf_op jit(solution)/shard_map/ppermute | solution.py:21
  462.8 5.7 collective-permute-start.20
  467.3 7.8 %collective-permute-start.23 = (f32[128,3,128]{2,1,0:T(4,128)S(1)}, f32[128,3,128]{2,1,0:T(4,128)S(1)}, u32[]{:S(2)}, u32[]{:S(2)}) collective-permute-start(f32[128,3,128]{2,1,0:T(4,128)S(1)} %get-tuple-element.25), channel_id=1, source_target_pairs={{0,1},{1,0},{2,3},{3,2},{4,5},{5,4},{6,7},{7,6},{8,9},{9,8},{10,11... | collective-permute-start | bytes 589832 | tf_op jit(solution)/shard_map/ppermute | solution.py:21
  467.5 9.0 %collective-permute-start.22 = (f32[128,3,128]{2,1,0:T(4,128)S(1)}, f32[128,3,128]{2,1,0:T(4,128)S(1)}, u32[]{:S(2)}, u32[]{:S(2)}) collective-permute-start(f32[128,3,128]{2,1,0:T(4,128)S(1)} %get-tuple-element.26), channel_id=1, source_target_pairs={{0,32},{8,40},{16,48},{24,56},{32,0},{40,8},{48,16},{56,24},{64,96... | collective-permute-start | bytes 589832 | tf_op jit(solution)/shard_map/ppermute | solution.py:21
  467.5 11.2 %collective-permute-start.21 = (f32[128,3,128]{2,1,0:T(4,128)S(1)}, f32[128,3,128]{2,1,0:T(4,128)S(1)}, u32[]{:S(2)}, u32[]{:S(2)}) collective-permute-start(f32[128,3,128]{2,1,0:T(4,128)S(1)} %get-tuple-element.27), channel_id=1, source_target_pairs={{0,16},{8,24},{16,0},{24,8},{32,48},{40,56},{48,32},{56,40},{64,80... | collective-permute-start | bytes 589832 | tf_op jit(solution)/shard_map/ppermute | solution.py:21
  509.7 0.9 copy-start.1
  519.5 11.3 %collective-permute-start.24 = (f32[128,3,128]{2,1,0:T(4,128)S(1)}, f32[128,3,128]{2,1,0:T(4,128)S(1)}, u32[]{:S(2)}, u32[]{:S(2)}) collective-permute-start(f32[128,3,128]{2,1,0:T(4,128)S(1)} %get-tuple-element.20), channel_id=1, source_target_pairs={{0,8},{8,0},{16,24},{24,16},{32,40},{40,32},{48,56},{56,48},{64,72... | collective-permute-start | bytes 589832 | tf_op jit(solution)/shard_map/ppermute | solution.py:21
  526.4 7.8 %collective-permute-start.27 = (f32[128,3,128]{2,1,0:T(4,128)S(1)}, f32[128,3,128]{2,1,0:T(4,128)S(1)}, u32[]{:S(2)}, u32[]{:S(2)}) collective-permute-start(f32[128,3,128]{2,1,0:T(4,128)S(1)} %get-tuple-element.21), channel_id=1, source_target_pairs={{0,1},{1,0},{2,3},{3,2},{4,5},{5,4},{6,7},{7,6},{8,9},{9,8},{10,11... | collective-permute-start | bytes 589832 | tf_op jit(solution)/shard_map/ppermute | solution.py:21
  526.4 9.0 %collective-permute-start.26 = (f32[128,3,128]{2,1,0:T(4,128)S(1)}, f32[128,3,128]{2,1,0:T(4,128)S(1)}, u32[]{:S(2)}, u32[]{:S(2)}) collective-permute-start(f32[128,3,128]{2,1,0:T(4,128)S(1)} %get-tuple-element.22), channel_id=1, source_target_pairs={{0,32},{8,40},{16,48},{24,56},{32,0},{40,8},{48,16},{56,24},{64,96... | collective-permute-start | bytes 589832 | tf_op jit(solution)/shard_map/ppermute | solution.py:21
  529.2 13.2 %collective-permute-start.25 = (f32[128,3,128]{2,1,0:T(4,128)S(1)}, f32[128,3,128]{2,1,0:T(4,128)S(1)}, u32[]{:S(2)}, u32[]{:S(2)}) collective-permute-start(f32[128,3,128]{2,1,0:T(4,128)S(1)} %get-tuple-element.23), channel_id=1, source_target_pairs={{0,16},{8,24},{16,0},{24,8},{32,48},{40,56},{48,32},{56,40},{64,80... | collective-permute-start | bytes 589832 | tf_op jit(solution)/shard_map/ppermute | solution.py:21
  551.1 106.0 %copy-start.2 = (f32[128,1536]{1,0:T(8,128)S(1)}, f32[128,1536]{1,0:T(8,128)}, u32[]{:S(2)}) copy-start(f32[128,1536]{1,0:T(8,128)} %copy-done.1) | copy-start | bytes 2359300
